TPU v7x, 32 devices: a whole 2x2x4 slice. The times are simulated.
32 devices in a mesh: mem: 8 (over z, y), band: 4 (over x, core).
Axes of the slice: x: 2, y: 2, z: 4, core: 2. Of those that a mesh axis runs over, the one named last changes fastest.
Arguments:
- alpha: bfloat16 [16, 4, 320, 720], P('mem', None, 'band'), may hold values from -6 to 6
- static_ctl: bfloat16 [4, 320, 720], P(None, 'band'), may hold values from -6 to 6
- perturbations: bfloat16 [16, 4, 320, 720], P('mem', None, None, 'band'), may hold values from -6 to 6
- static_std: float32 [4, 320, 720], P(None, None, 'band'), may hold values from 0.5 to 2
- lon_root: bfloat16 [720, 720], replicated, may hold values from -0.11 to 1.11
- lat_root: bfloat16 [320, 320], replicated, may hold values from -0.11 to 1.11
- jacobian: bfloat16 [32, 4, 320, 720], P(None, None, 'mem', 'band'), may hold values from -3 to 3
- obs_count: int32 [320, 720], P('mem', 'band'), may hold values from 1 to 6
- channel_mask: int32 [32, 320, 720], P(None, 'mem', 'band'), may hold values 0 or 1
- channel_error: float32 [32], replicated, may hold values from 1 to 2
- member_weight: int32 [16], replicated, may hold values from 1 to 4
Outputs:
- grad_alpha: float32 [16, 4, 320, 720], P('mem', None, 'band')
- grad_static: float32 [4, 320, 720], P(None, 'band')
All inputs are finite; a program needn't handle non-finite values. No bound on the sum of `channel_mask` on one device may be relied on, other than what follows from the above.
Results may differ from a plain program's by a relative error of at most 0.0055.
Values may be sent and summed in bfloat16 or wider, within the bound.
No kernel may reach another device: no remote copies, remote signals or barrier semaphores. Data moves between devices by JAX's collectives and lax.ppermute only.
A program may use at most 64 MiB of HBM per device.

v0:
```python
import jax
import jax.numpy as jnp
from jax import lax
from jax.sharding import PartitionSpec as P


def shards(
    alpha,
    static_ctl,
    perturbations,
    static_std,
    lon_root,
    lat_root,
    jacobian,
    obs_count,
    channel_mask,
    channel_error,
    member_weight,
):
    members = alpha.shape[0]
    rows = jacobian.shape[2]
    rank = lax.axis_index("mem")
    weights = member_weight.astype(jnp.float32)
    coef = weights / jnp.sqrt(jnp.sum(weights * weights))
    own_coef = lax.dynamic_slice_in_dim(coef, rank * members, members, 0)
    fields = jnp.concatenate([alpha, static_ctl[None]], axis=0)
    along_lon = jnp.dot(fields, lon_root, preferred_element_type=jnp.float32).astype(jnp.bfloat16)
    regrouped = lax.all_to_all(along_lon, "band", split_axis=3, concat_axis=2, tiled=True)
    member_lat = jnp.einsum(
        "ij,msjk->msik", lat_root, regrouped[:members], preferred_element_type=jnp.float32
    )
    own_root = lax.dynamic_slice_in_dim(lat_root, rank * rows, rows, 0)
    own_static = jnp.einsum(
        "ij,sjk->sik", own_root, regrouped[members], preferred_element_type=jnp.float32
    )
    scaled = 0.8 * own_coef
    ensemble_term = jnp.sum(
        scaled[:, None, None, None] * perturbations.astype(jnp.float32) * member_lat, axis=0
    )
    summed = lax.psum(ensemble_term, "mem")
    own_sum = lax.dynamic_slice_in_dim(summed, rank * rows, rows, 1)
    own_std = lax.dynamic_slice_in_dim(static_std, rank * rows, rows, 1)
    increment = own_sum + 0.6 * own_std * own_static
    obs_weight = (
        channel_mask.astype(jnp.float32)
        * obs_count.astype(jnp.float32)[None]
        / (channel_error * channel_error)[:, None, None]
    )
    jac_full = jacobian.astype(jnp.float32)
    radiance = jnp.sum(jac_full * increment[None], axis=1)
    obs_gradient = jnp.sum(jac_full * (obs_weight * radiance)[:, None], axis=0).astype(jnp.bfloat16)
    band_gradient = lax.all_gather(obs_gradient, "mem", axis=1, tiled=True).astype(jnp.float32)
    member_adjoint = (
        scaled[:, None, None, None] * perturbations.astype(jnp.float32) * band_gradient[None]
    ).astype(jnp.bfloat16)
    static_adjoint = (0.6 * static_std * band_gradient).astype(jnp.bfloat16)
    adjoints = jnp.concatenate([member_adjoint, static_adjoint[None]], axis=0)
    back_lat = jnp.einsum(
        "ji,msjk->msik", lat_root, adjoints, preferred_element_type=jnp.float32
    ).astype(jnp.bfloat16)
    returned = lax.all_to_all(back_lat, "band", split_axis=2, concat_axis=3, tiled=True)
    back_lon = jnp.einsum("msil,jl->msij", returned, lon_root, preferred_element_type=jnp.float32)
    grad_alpha = alpha.astype(jnp.float32) + back_lon[:members]
    grad_static = static_ctl.astype(jnp.float32) + back_lon[members]
    return (grad_alpha, grad_static)


def solution(mesh):
    in_specs = (
        P("mem", None, "band", None),
        P(None, "band", None),
        P("mem", None, None, "band"),
        P(None, None, "band"),
        P(),
        P(),
        P(None, None, "mem", "band"),
        P("mem", "band"),
        P(None, "mem", "band"),
        P(),
        P(),
    )
    out_specs = (P("mem", None, "band", None), P(None, "band", None))
    return jax.shard_map(shards, mesh=mesh, in_specs=in_specs, out_specs=out_specs, check_vma=False)
```

profile of v0, /device:TPU:0, one launch (start us, length us, event | category | flops | bytes accessed | tf_op | source)
XLA Modules:
  0.0 232.6 jit_solution(4130602733582369304)
XLA Ops:
  7.2 1.2 copy-done
  8.4 2.7 %convolution_convert_fusion.1 = bf16[3,4,80,720]{3,2,1,0:T(8,128)(2,1)S(1)} fusion(bf16[1,4,80,720]{3,2,1,0:T(8,128)(2,1)} %bitcast.52, bf16[2,4,80,720]{3,2,1,0:T(8,128)(2,1)} %param.11, bf16[720,720]{1,0:T(8,128)(2,1)S(1)} %copy-done), kind=kOutput, calls=%fused_computation.13 | convolution fusion | flops 996710400 | bytes 3801600 | tf_op jit(solution)/shard_map/dot_general | solution.py:27
  11.1 3.3 %copy.28 = bf16[3,4,80,720]{2,1,0,3:T(4,128)(2,1)} copy(bf16[3,4,80,720]{3,2,1,0:T(8,128)(2,1)S(1)} %convolution_convert_fusion.1) | data formatting | bytes 2764800 | tf_op jit(solution)/shard_map/convert_element_type | solution.py:27
  14.4 4.4 %all-to-all-start = ((bf16[3,4,80,720]{2,1,0,3:T(4,128)(2,1)}), bf16[3,4,80,720]{2,1,0,3:T(4,128)(2,1)S(1)}, u32[]{:S(2)}, u32[]{:S(2)}) async-start(bf16[3,4,80,720]{2,1,0,3:T(4,128)(2,1)} %copy.28), calls=%async_computation | async-start | bytes 4423680 | tf_op jit(solution)/shard_map/all_to_all | solution.py:28
  18.7 0.6 multiply_reduce_fusion
  20.1 25.5 %all-to-all-done = bf16[3,4,80,720]{2,1,0,3:T(4,128)(2,1)S(1)} async-done(((bf16[3,4,80,720]{2,1,0,3:T(4,128)(2,1)}), bf16[3,4,80,720]{2,1,0,3:T(4,128)(2,1)S(1)}, u32[]{:S(2)}, u32[]{:S(2)}) %all-to-all-start) | async-done | bytes 1382432 | tf_op jit(solution)/shard_map/all_to_all | solution.py:28
  45.6 3.8 %copy.29 = bf16[3,4,80,4,180]{4,2,3,1,0:T(8,128)(2,1)} copy(bf16[3,4,80,4,180]{2,1,0,4,3:T(4,128)(2,1)S(1)} %bitcast.46) | data formatting | bytes 2764800 | tf_op jit(solution)/shard_map/all_to_all | solution.py:28
  49.4 1.5 slice.21
  51.1 1.4 fusion.2
  52.5 1.5 copy.31
  54.1 0.3 constant_dynamic-slice_fusion
  54.6 1.1 slice.22
  55.7 83.2 %all-reduce.2.cloned.1.call-done = f32[4,320,180]{2,1,0:T(8,128)} async-done(((f32[4,320,180]{2,1,0:T(8,128)}), f32[4,320,180]{2,1,0:T(8,128)}) %all-reduce.2.cloned.1.call-update) | async-done | bytes 921616 | tf_op jit(solution)/shard_map/psum | solution.py:40
  138.9 1.2 fusion.13
  140.1 2.6 %fusion = f32[32,40,180]{2,1,0:T(8,128)S(1)} fusion(bf16[32,4,40,180]{3,2,1,0:T(8,128)(2,1)} %param.17, f32[4,40,180]{2,1,0:T(8,128)S(1)} %fusion.13), kind=kLoop, calls=%fused_computation.2 | loop fusion | flops 2534400 | bytes 2880000 | tf_op jit(solution)/shard_map/reduce_sum | solution.py:50
  143.0 1.5 copy-done.1
  144.5 0.7 fusion.1
  145.2 31.8 %all_gather.3 = bf16[4,320,180]{2,0,1:T(4,128)(2,1)S(1)} all-gather(bf16[4,40,180]{2,0,1:T(4,128)(2,1)S(1)} %copy.34), channel_id=1, replica_groups=mesh['mem'=8,'band'=4] {'mem'}, dimensions={1}, use_global_device_ids=true | all-gather | bytes 518400 | tf_op jit(solution)/shard_map/all_gather | solution.py:52
  177.0 0.9 copy.35
  178.1 1.0 copy-done.5
  179.1 0.4 multiply_convert_fusion
  179.5 0.6 copy-done.10
  180.0 2.5 %fusion.6 = bf16[3,4,320,180]{2,3,1,0:T(8,128)(2,1)} fusion(bf16[1,4,320,180]{2,3,1,0:T(8,128)(2,1)S(1)} %fusion.20, bf16[2,4,320,180]{2,3,1,0:T(8,128)(2,1)S(1)} %multiply_convert_fusion, bf16[320,320]{1,0:T(8,128)(2,1)S(1)} %copy-done.10), kind=kOutput, calls=%fused_computation.14 | convolution fusion | flops 443750400 | bytes 2969600 | tf_op jit(solution)/shard_map/ji,msjk->msik/dot_general | solution.py:58
  182.6 6.7 %copy.37 = bf16[3,4,320,180]{3,1,0,2:T(4,128)(2,1)S(1)} copy(bf16[3,4,320,180]{2,3,1,0:T(8,128)(2,1)} %fusion.6) | data formatting | bytes 2764800 | tf_op jit(solution)/shard_map/convert_element_type | solution.py:60
  189.2 26.8 %all_to_all.33 = bf16[3,4,320,180]{3,1,0,2:T(4,128)(2,1)S(1)} all-to-all(bf16[3,4,320,180]{3,1,0,2:T(4,128)(2,1)S(1)} %copy.37), channel_id=1, replica_groups=mesh['mem'=8,'band'=4] {'band'}, dimensions={2} | all-to-all | bytes 2764800 | tf_op jit(solution)/shard_map/all_to_all | solution.py:61
  216.0 0.3 copy.38
  216.3 1.0 copy.39
  217.4 2.5 %all_to_all.30 = bf16[3,4,80,720]{3,2,1,0:T(8,128)(2,1)} reshape(bf16[3,4,80,4,180]{4,3,2,1,0:T(4,128)(2,1)S(1)} %copy.39) | data formatting | bytes 2764800 | tf_op jit(solution)/shard_map/all_to_all | solution.py:61
  219.9 2.8 %fusion.16 = f32[3,4,80,720]{3,2,1,0:T(8,128)S(1)} fusion(bf16[3,4,80,720]{3,2,1,0:T(8,128)(2,1)} %all_to_all.30, bf16[720,720]{1,0:T(8,128)(2,1)S(1)} %copy-done), kind=kOutput, calls=%fused_computation.25 | convolution fusion | flops 995328000 | bytes 5184000 | tf_op jit(solution)/shard_map/msil,jl->msij/dot_general | solution.py:62
  222.7 1.0 fusion.19
  223.7 0.5 copy-done.6
  224.2 1.5 slice_add_fusion
  (32 shorter events, 1.1 us)
Async XLA Ops:
  7.2 1.3 copy-start
  14.4 4.4 %copy-start.11 = (s32[16]{0:T(128)S(1)}, s32[16]{0:T(128)}, u32[]{:S(2)}) copy-start(s32[16]{0:T(128)} %param.21) | copy-start | bytes 196
  14.4 31.3 %all-to-all-start = ((bf16[3,4,80,720]{2,1,0,3:T(4,128)(2,1)}), bf16[3,4,80,720]{2,1,0,3:T(4,128)(2,1)S(1)}, u32[]{:S(2)}, u32[]{:S(2)}) async-start(bf16[3,4,80,720]{2,1,0,3:T(4,128)(2,1)} %copy.28), calls=%async_computation | async-start | bytes 4423680 | tf_op jit(solution)/shard_map/all_to_all | solution.py:28
  18.7 120.2 %all-reduce.2.cloned.1.call-start = ((), (), s32[]{:S(2)}) async-start(), calls=%async_computation.2 | async-start | bytes 2621440 | tf_op jit(solution)/shard_map/psum | solution.py:40
  49.4 1.6 copy-start.4
  49.4 1.7 copy-start.9
  52.4 1.6 copy-start.12
  52.4 1.6 copy-start.8
  52.5 1.6 copy-start.2
  140.1 2.7 %copy-start.3 = (s32[32,40,180]{2,1,0:T(8,128)S(1)}, s32[32,40,180]{2,1,0:T(8,128)}, u32[]{:S(2)}) copy-start(s32[32,40,180]{2,1,0:T(8,128)} %param.19) | copy-start | bytes 2764804
  142.8 1.7 copy-start.1
  177.8 1.2 copy-start.5
  179.1 0.9 copy-start.10
  219.9 2.8 %copy-start.7 = (bf16[4,80,720]{2,1,0:T(8,128)(2,1)S(1)}, bf16[4,80,720]{2,1,0:T(8,128)(2,1)}, u32[]{:S(2)}) copy-start(bf16[4,80,720]{2,1,0:T(8,128)(2,1)} %param.12) | copy-start | bytes 1382404
  222.7 1.6 copy-start.6
Sparse Core Ops, SparseCore 0:
  54.1 84.7 all-reduce.1
where the time goes:
time: 233 us
  waiting for transfers between devices  109 us (47%)
  blocking collectives  58.6 us (25%)
  local copies, waits for them, and re-layouts  28 us (12%)
  between operations  15 us (6%)
  matrix products  10.5 us (5%)
  other arithmetic  7.4 us (3%)
  starting transfers between devices  4.37 us (2%)
    psum x1, waiting for transfers between devices, shards(): summed = lax.psum(ensemble_term, 'mem')  83.2 us
    all_gather x1, blocking collectives, shards(): lax.all_gather(obs_gradient, 'mem', axis=1, tiled=True).astype(jnp.float32)  31.8 us
    all_to_all x1, blocking collectives, shards(): lax.all_to_all(back_lat, 'band', split_axis=2, concat_axis=3, tiled=True)  26.8 us
    all_to_all x1, waiting for transfers between devices, shards(): lax.all_to_all(along_lon, 'band', split_axis=3, concat_axis=2, tiled=True)  25.5 us
    convert_element_type x1, local copies, waits for them, and re-layouts, shards(): back_lat = jnp.einsum('ji,msjk->msik', lat_root, adjoints, preferred_elem...  6.66 us
    unnamed x27, local copies, waits for them, and re-layouts  5.19 us
  transfers between devices with their start and end apart: 2, of which 2 were waited for; matrix products, arithmetic and copies ran while one was open for 1% of the time, Pallas kernels for 0%

commit v1 on v0

--- a/solution.py
+++ b/solution.py
@@ -37,7 +37,7 @@
     ensemble_term = jnp.sum(
         scaled[:, None, None, None] * perturbations.astype(jnp.float32) * member_lat, axis=0
     )
-    summed = lax.psum(ensemble_term, "mem")
+    summed = jnp.sum(lax.all_gather(ensemble_term, "mem"), axis=0)
     own_sum = lax.dynamic_slice_in_dim(summed, rank * rows, rows, 1)
     own_std = lax.dynamic_slice_in_dim(static_std, rank * rows, rows, 1)
     increment = own_sum + 0.6 * own_std * own_static

time: 233 us -> 286 us (1.23)
  waiting for transfers between devices: 109 us -> 156 us
  other arithmetic: 7.4 us -> 11.6 us
    all_gather x0 -> x1, waiting for transfers between devices: none -> 131 us  [shards(): summed = jnp.sum(lax.all_gather(ensemble_term, 'mem'), axis=0)]
    psum x1 -> x0, waiting for transfers between devices: 83.2 us -> none  [shards(): summed = lax.psum(ensemble_term, 'mem')]
    reduce_sum x0 -> x1, other arithmetic: none -> 4.24 us  [shards(): summed = jnp.sum(lax.all_gather(ensemble_term, 'mem'), axis=0)]
where the time goes in v1:
time: 286 us
  waiting for transfers between devices  156 us (55%)
  blocking collectives  58.8 us (21%)
  local copies, waits for them, and re-layouts  27.9 us (10%)
  between operations  14.9 us (5%)
  other arithmetic  11.6 us (4%)
  matrix products  11.3 us (4%)
  starting transfers between devices  4.37 us (2%)
    all_gather x1, waiting for transfers between devices, shards(): summed = jnp.sum(lax.all_gather(ensemble_term, 'mem'), axis=0)  131 us
    all_gather x1, blocking collectives, shards(): lax.all_gather(obs_gradient, 'mem', axis=1, tiled=True).astype(jnp.float32)  32 us
    all_to_all x1, blocking collectives, shards(): lax.all_to_all(back_lat, 'band', split_axis=2, concat_axis=3, tiled=True)  26.8 us
    all_to_all x1, waiting for transfers between devices, shards(): lax.all_to_all(along_lon, 'band', split_axis=3, concat_axis=2, tiled=True)  25.5 us
    convert_element_type x1, local copies, waits for them, and re-layouts, shards(): back_lat = jnp.einsum('ji,msjk->msik', lat_root, adjoints, preferred_elem...  6.66 us
  transfers between devices with their start and end apart: 2, of which 2 were waited for; matrix products, arithmetic and copies ran while one was open for 1% of the time, Pallas kernels for 0%

profile of v1, /device:TPU:0, one launch (start us, length us, event | category | flops | bytes accessed | tf_op | source)
XLA Modules:
  0.0 285.5 jit_solution(7295096636082831438)
XLA Ops:
  7.2 1.2 copy-done
  8.4 2.7 convolution_convert_fusion.1
  11.1 3.3 %copy.40 = bf16[3,4,80,720]{2,1,0,3:T(4,128)(2,1)} copy(bf16[3,4,80,720]{3,2,1,0:T(8,128)(2,1)S(1)} %convolution_convert_fusion.1) | data formatting | bytes 2764800 | tf_op jit(solution)/shard_map/convert_element_type | solution.py:27
  14.4 4.4 %all-to-all-start = ((bf16[3,4,80,720]{2,1,0,3:T(4,128)(2,1)}), bf16[3,4,80,720]{2,1,0,3:T(4,128)(2,1)S(1)}, u32[]{:S(2)}, u32[]{:S(2)}) async-start(bf16[3,4,80,720]{2,1,0,3:T(4,128)(2,1)} %copy.40), calls=%async_computation | async-start | bytes 4423680 | tf_op jit(solution)/shard_map/all_to_all | solution.py:28
  18.7 0.6 multiply_reduce_fusion
  20.1 25.5 %all-to-all-done = bf16[3,4,80,720]{2,1,0,3:T(4,128)(2,1)S(1)} async-done(((bf16[3,4,80,720]{2,1,0,3:T(4,128)(2,1)}), bf16[3,4,80,720]{2,1,0,3:T(4,128)(2,1)S(1)}, u32[]{:S(2)}, u32[]{:S(2)}) %all-to-all-start) | async-done | bytes 1382432 | tf_op jit(solution)/shard_map/all_to_all | solution.py:28
  45.6 3.8 %copy.41 = bf16[3,4,80,4,180]{4,2,3,1,0:T(8,128)(2,1)} copy(bf16[3,4,80,4,180]{2,1,0,4,3:T(4,128)(2,1)S(1)} %bitcast.48) | data formatting | bytes 2764800 | tf_op jit(solution)/shard_map/all_to_all | solution.py:28
  49.4 1.5 slice.21
  51.1 2.4 fusion.2
  53.5 1.4 constant_dynamic-slice_fusion
  55.1 1.1 slice.22
  56.2 131.0 %all-gather.3.cloned.1.call-done = f32[32,320,180]{1,2,0:T(8,128)} async-done(((f32[4,320,180]{1,2,0:T(8,128)}), f32[32,320,180]{1,2,0:T(8,128)}) %all-gather.3.cloned.1.call-update) | async-done | bytes 7372816 | tf_op jit(solution)/shard_map/all_gather | solution.py:40
  187.2 4.2 %reduce_sum.47 = f32[4,320,180]{1,2,0:T(8,128)S(1)} reduce(f32[8,4,320,180]{2,3,1,0:T(8,128)} %bitcast.47, f32[]{:T(128)} %constant.10.clone.1), dimensions={0}, to_apply=%region_2.0 | reduce | flops 1612800 | bytes 8294404 | tf_op jit(solution)/shard_map/reduce_sum | solution.py:40
  191.8 1.0 fusion.13
  192.8 2.6 fusion
  195.7 1.5 copy-done.1
  197.2 0.7 fusion.1
  197.9 32.0 %all_gather.11 = bf16[4,320,180]{2,0,1:T(4,128)(2,1)S(1)} all-gather(bf16[4,40,180]{2,0,1:T(4,128)(2,1)S(1)} %copy.46), channel_id=1, replica_groups=mesh['mem'=8,'band'=4] {'mem'}, dimensions={1}, use_global_device_ids=true | all-gather | bytes 518400 | tf_op jit(solution)/shard_map/all_gather | solution.py:52
  229.9 0.9 copy.47
  231.1 1.0 copy-done.5
  232.0 0.4 multiply_convert_fusion
  232.4 0.6 copy-done.10
  233.0 2.5 fusion.6
  235.5 6.7 %copy.49 = bf16[3,4,320,180]{3,1,0,2:T(4,128)(2,1)S(1)} copy(bf16[3,4,320,180]{2,3,1,0:T(8,128)(2,1)} %fusion.6) | data formatting | bytes 2764800 | tf_op jit(solution)/shard_map/convert_element_type | solution.py:60
  242.2 26.8 %all_to_all.33 = bf16[3,4,320,180]{3,1,0,2:T(4,128)(2,1)S(1)} all-to-all(bf16[3,4,320,180]{3,1,0,2:T(4,128)(2,1)S(1)} %copy.49), channel_id=1, replica_groups=mesh['mem'=8,'band'=4] {'band'}, dimensions={2} | all-to-all | bytes 2764800 | tf_op jit(solution)/shard_map/all_to_all | solution.py:61
  269.0 0.3 copy.50
  269.3 1.0 copy.51
  270.3 2.5 all_to_all.30
  272.8 2.8 fusion.16
  275.6 1.0 fusion.19
  276.7 0.5 copy-done.6
  277.2 1.5 slice_add_fusion
  (34 shorter events, 1.4 us)
Async XLA Ops:
  7.2 1.3 copy-start
  14.4 4.4 %copy-start.11 = (s32[16]{0:T(128)S(1)}, s32[16]{0:T(128)}, u32[]{:S(2)}) copy-start(s32[16]{0:T(128)} %param.21) | copy-start | bytes 196
  14.4 31.3 %all-to-all-start = ((bf16[3,4,80,720]{2,1,0,3:T(4,128)(2,1)}), bf16[3,4,80,720]{2,1,0,3:T(4,128)(2,1)S(1)}, u32[]{:S(2)}, u32[]{:S(2)}) async-start(bf16[3,4,80,720]{2,1,0,3:T(4,128)(2,1)} %copy.40), calls=%async_computation | async-start | bytes 4423680 | tf_op jit(solution)/shard_map/all_to_all | solution.py:28
  18.7 168.5 %all-gather.3.cloned.1.call-start = ((), (), s32[]{:S(2)}) async-start(), calls=%async_computation.2 | async-start | bytes 10174464 | tf_op jit(solution)/shard_map/all_gather | solution.py:40
  49.4 1.6 copy-start.4
  49.4 1.7 copy-start.9
  51.1 2.4 copy-start.12
  51.1 2.4 copy-start.8
  192.8 2.7 copy-start.3
  195.5 1.7 copy-start.1
  197.9 32.9 %copy-start.2 = (f32[4,320,180]{1,0,2:T(4,128)S(1)}, f32[4,320,180]{1,0,2:T(4,128)}, u32[]{:S(2)}) copy-start(f32[4,320,180]{1,0,2:T(4,128)} %param.14) | copy-start | bytes 2764804
  230.8 1.2 copy-start.5
  232.0 0.9 copy-start.10
  272.8 2.8 copy-start.7
  275.6 1.6 copy-start.6
Sparse Core Ops, SparseCore 0:
  53.6 133.5 all-gather.2
